TPU v7x, 32 devices: a whole 2x2x4 slice. The times are simulated.
32 devices in a mesh: req: 16 (over z, y, x), tp: 2 (over core).
Axes of the slice: x: 2, y: 2, z: 4, core: 2. Of those that a mesh axis runs over, the one named last changes fastest.
Arguments:
- tokens: bfloat16 [8192, 3072], P('req', 'tp'), may hold values from -6 to 6
- norm_gain: bfloat16 [3072], P('tp'), may hold values from 0.099609375 to 1.8984375
- qkv_weight: bfloat16 [3, 3072, 3072], P(None, 'req', 'tp'), may hold values from -0.109375 to 0.109375
- out_weight: bfloat16 [3072, 3072], P('tp', 'req'), may hold values from -1.75 to 1.75
- cache: bfloat16 [16, 2, 2048, 3072], P('req', None, None, 'tp'), may hold values from -720 to 720
- cache_lens: int32 [16], P('req'), may hold values from 0 to 2048, as said below
- valid_tokens: int32 [16], P('req'), may hold values from 128 to 512, as said below
Outputs:
- mixed: bfloat16 [8192, 3072], P('req', 'tp')
- new_entries: bfloat16 [16, 2, 512, 3072], P('req', None, None, 'tp')
Inputs may be any that keep to these rules, and one draw needn't show every extreme that they name: `cache_lens`: in every draw some request's cache holds all 2048 entries and some request's cache is empty. `valid_tokens`: in every draw some request brings 512 live new tokens.
All inputs are finite; a program needn't handle non-finite values.
Results may differ from a plain program's by a relative error of at most 0.0095.
The roundings to bfloat16 on the way count: a program that leaves them out, or rounds other values in their place, can miss the bound.
Values may be sent and summed in bfloat16 or wider, within the bound.
A program may use at most 192 MiB of HBM per device.

v0:
```python
import math

import jax
import jax.numpy as jnp
from jax import lax
from jax.sharding import PartitionSpec as P

HD = 96


epsilon = 1e-05
masked_value = -1e30
theta_base = 10000.0


def rotate(projected, positions):
    tokens_here, columns = projected.shape
    per_head = projected.reshape(tokens_here, columns // HD, HD)
    frequencies = jnp.power(theta_base, -jnp.arange(0, HD, 2, dtype=jnp.float32) / HD)
    angles = positions.astype(jnp.float32)[:, None] * frequencies[None, :]
    cosine = jnp.cos(angles)[:, None, :]
    sine_table = jnp.sin(angles)[:, None, :]
    first_half = per_head[..., : HD // 2]
    second_half = per_head[..., HD // 2 :]
    turned = jnp.concatenate(
        [
            first_half * cosine - second_half * sine_table,
            second_half * cosine + first_half * sine_table,
        ],
        axis=-1,
    )
    return turned.reshape(tokens_here, columns)


def add_rows(source, piece):
    return jnp.einsum("td,jdc->jtc", source, piece, preferred_element_type=jnp.float32)


def score_block(queries, key_rows, score_scale):
    return (
        lax.dot_general(
            queries, key_rows, (((1,), (1,)), ((), ())), preferred_element_type=jnp.float32
        )
        * score_scale
    )


def attend_whole(
    queries, cache_keys, cache_values, keys_new, values_new, length, live_mask, score_scale
):
    cache_scores = score_block(queries, cache_keys, score_scale)
    cache_ids = jnp.arange(cache_keys.shape[0], dtype=jnp.int32)
    cache_scores = jnp.where((cache_ids < length)[None, :], cache_scores, masked_value)
    new_scores = jnp.where(live_mask, score_block(queries, keys_new, score_scale), masked_value)
    scores = jnp.concatenate([cache_scores, new_scores], axis=1)
    maximum = jnp.max(scores, axis=1, keepdims=True)
    expo = jnp.exp(scores - maximum)
    weights = (expo / jnp.sum(expo, axis=1, keepdims=True)).astype(jnp.bfloat16)
    value_rows = jnp.concatenate([cache_values, values_new], axis=0)
    return jnp.dot(weights, value_rows, preferred_element_type=jnp.float32).astype(jnp.bfloat16)


def attend_all(
    queries, keys_new, values_new, cache_keys, cache_values, length, live_mask, score_scale
):
    query_rows, head_cols = queries.shape

    def per_head(head_index):
        col_start = head_index * HD

        def select(source):
            return lax.dynamic_slice_in_dim(source, col_start, HD, 1)

        return attend_whole(
            select(queries),
            select(cache_keys),
            select(cache_values),
            select(keys_new),
            select(values_new),
            length,
            live_mask,
            score_scale,
        )

    heads_out = lax.map(per_head, jnp.arange(head_cols // HD, dtype=jnp.int32))
    return jnp.transpose(heads_out, (1, 0, 2)).reshape(query_rows, head_cols)


def per_device(tokens, norm_gain, qkv_weight, out_weight, cache, cache_lens, valid_tokens):
    gathered, gain_all = (
        lax.all_gather(tokens, "tp", axis=1, tiled=True),
        lax.all_gather(norm_gain, "tp", axis=0, tiled=True),
    )
    inputs = gathered.astype(jnp.float32)
    spread = jnp.mean(inputs * inputs, axis=-1, keepdims=True)
    normed = (inputs * lax.rsqrt(spread + epsilon) * gain_all.astype(jnp.float32)).astype(
        jnp.bfloat16
    )
    new_rows = normed.shape[0]
    length = cache_lens[0]
    valid_count = valid_tokens[0]
    token_ids = jnp.arange(new_rows, dtype=jnp.int32)
    positions = length + token_ids
    projected = add_rows(normed, lax.all_gather(qkv_weight, "req", axis=1, tiled=True))
    combined = jnp.stack(
        [rotate(projected[0], positions), rotate(projected[1], positions), projected[2]]
    ).astype(jnp.bfloat16)
    queries = combined[0]
    keys_new = combined[1]
    values_new = combined[2]
    kept = (token_ids < valid_count)[:, None]
    new_entries = jnp.stack(
        [
            jnp.where(kept, keys_new, jnp.zeros_like(keys_new)),
            jnp.where(kept, values_new, jnp.zeros_like(values_new)),
        ]
    )[None]
    live_mask = (token_ids[None, :] <= token_ids[:, None]) & (token_ids[None, :] < valid_count)
    cache_keys = cache[0, 0]
    cache_values = cache[0, 1]
    score_scale = 1.0 / math.sqrt(HD)
    attended = attend_all(
        queries, keys_new, values_new, cache_keys, cache_values, length, live_mask, score_scale
    )
    partial_value = jnp.dot(
        attended,
        lax.all_gather(out_weight, "req", axis=1, tiled=True),
        preferred_element_type=jnp.float32,
    )
    summed = lax.psum_scatter(
        partial_value.astype(jnp.bfloat16), "tp", scatter_dimension=1, tiled=True
    ).astype(jnp.float32)
    mixed_out = jnp.where(kept, summed, jnp.zeros_like(summed)).astype(jnp.bfloat16)
    return (mixed_out, new_entries)


def solution(mesh):
    placed = (
        P("req", "tp"),
        P("tp"),
        P(None, "req", "tp"),
        P("tp", "req"),
        P("req", None, None, "tp"),
        P("req"),
        P("req"),
    )
    return jax.shard_map(
        per_device,
        mesh=mesh,
        in_specs=placed,
        out_specs=(P("req", "tp"), P("req", None, None, "tp")),
        check_vma=False,
    )
```

profile of v0, /device:TPU:0, one launch (start us, length us, event | category | flops | bytes accessed | tf_op | source)
XLA Modules:
  0.0 568.6 jit_solution(8117036062014066321)
XLA Ops:
  9.5 1.9 all-gather
  12.8 10.4 %slice_bitcast_fusion = (bf16[2048,1536]{1,0:T(8,128)(2,1)}, bf16[2048,1536]{1,0:T(8,128)(2,1)}) fusion(bf16[1,2,2048,1536]{3,2,1,0:T(8,128)(2,1)} %param.13), kind=kLoop, calls=%fused_computation.33 | loop fusion | bytes 25165824 | tf_op jit(solution)/shard_map/squeeze | solution.py:120
  24.4 2.7 fusion.21
  27.1 302.5 %all-gather.7.cloned.1.call-done = bf16[3,3072,1536]{2,1,0:T(8,128)(2,1)} async-done(((bf16[3,192,1536]{2,1,0:T(8,128)(2,1)}), bf16[3,3072,1536]{2,1,0:T(8,128)(2,1)}) %all-gather.7.cloned.1.call-update) | async-done | bytes 28311568 | tf_op jit(solution)/shard_map/all_gather | solution.py:104
  329.6 19.0 %convolution_bitcast_fusion = f32[3,512,1536]{2,1,0:T(8,128)S(1)} fusion(bf16[3,3072,1536]{2,1,0:T(8,128)(2,1)} %all-gather.7.cloned.1.call-done, bf16[512,3072]{1,0:T(8,128)(2,1)S(1)} %copy-done.3, f32[3072]{0:T(1024)S(1)} %bitcast.43, f32[512]{0:T(512)S(1)} %add_rsqrt_fusion), kind=kOutput, calls=%fused_computation.35 | convolution fusion | flops 14501806080 | bytes 40908800 | tf_op jit(solution)/shard_map/td,jdc->jtc/dot_general | solution.py:36
  348.6 3.4 fusion.31
  352.1 2.1 copy-done
  354.1 2.4 copy.17
  356.5 3.5 copy.18
  360.0 3.4 subtract_convert_fusion
  365.5 4.4 broadcast_select_fusion
  369.9 170.7 %while.11 = (s32[]{:T(128)}, bf16[16,512,96]{1,2,0:T(8,128)(2,1)}, s32[]{:T(128)}, s32[16]{0:T(128)S(1)}, bf16[512,1536]{0,1:T(8,128)(2,1)}, /*index=5*/bf16[204...) while((s32[]{:T(128)}, bf16[16,512,96]{1,2,0:T(8,128)(2,1)}, ...), condition=%wide.region_5.6_spmd.clone, body=%wide.region_1.5_spmd.clone.sunk | while | flops 517981184 | bytes 18146508 | solution.py:85
  371.7 2.3 fusion.42
  378.7 2.0 fusion.44
  382.4 2.3 fusion.42
  389.4 2.0 fusion.44
  393.1 2.3 fusion.42
  400.1 2.0 fusion.44
  403.8 2.3 fusion.42
  410.8 2.0 fusion.44
  414.5 2.3 fusion.42
  421.5 2.0 fusion.44
  425.2 2.3 fusion.42
  432.2 2.0 fusion.44
  435.9 2.3 fusion.42
  442.9 2.0 fusion.44
  446.6 2.3 fusion.42
  453.6 2.0 fusion.44
  457.3 2.3 fusion.42
  464.2 2.0 fusion.44
  468.0 2.3 fusion.42
  474.9 2.0 fusion.44
  478.7 2.3 fusion.42
  485.6 2.0 fusion.44
  489.3 2.3 fusion.42
  496.3 2.0 fusion.44
  500.0 2.3 fusion.42
  507.0 2.0 fusion.44
  510.7 2.3 fusion.42
  517.7 2.0 fusion.44
  521.4 2.3 fusion.42
  528.4 2.0 fusion.44
  532.1 2.1 fusion.42
  538.6 2.0 fusion.44
  540.6 9.4 %convolution_convert_fusion = bf16[512,3072]{1,0:T(8,128)(2,1)} fusion(bf16[512,1536]{0,1:T(8,128)(2,1)} %bitcast.44, bf16[1536,3072]{0,1:T(8,128)(2,1)} %all-gather.9.cloned.1.call-done), kind=kOutput, calls=%fused_computation.36 | convolution fusion | flops 4833411072 | bytes 14155776 | tf_op jit(solution)/shard_map/dot_general | solution.py:125
  551.9 1.9 maximum_bitcast_fusion
  553.9 5.3 reduce-scatter.2.cloned.1.call-done
  559.2 2.9 select_convert_fusion
  (142 shorter events, 101.2 us)
Async XLA Ops:
  7.2 2.3 copy-start.4
  7.2 17.2 %all-gather.5.cloned.1.call-start = ((), (), s32[]{:S(2)}) async-start(), calls=%async_computation.1 | async-start | bytes 4718592 | tf_op jit(solution)/shard_map/all_gather | solution.py:91
  7.9 321.7 %all-gather.7.cloned.1.call-start = ((), (), s32[]{:S(2)}) async-start(), calls=%async_computation.2 | async-start | bytes 30081024 | tf_op jit(solution)/shard_map/all_gather | solution.py:104
  8.7 532.0 %all-gather.9.cloned.1.call-start = ((), (), s32[]{:S(2)}) async-start(), calls=%async_computation.3 | async-start | bytes 10027008 | tf_op jit(solution)/shard_map/all_gather | solution.py:127
  9.4 549.8 %reduce-scatter.2.cloned.1.call-start = ((), (), s32[]{:S(2)}) async-start(), calls=%async_computation.4 | async-start | bytes 4718592 | tf_op jit(solution)/shard_map/reduce_scatter | solution.py:130
  24.4 305.2 %copy-start.3 = (bf16[512,3072]{1,0:T(8,128)(2,1)S(1)}, bf16[512,3072]{1,0:T(8,128)(2,1)}, u32[]{:S(2)}) copy-start(bf16[512,3072]{1,0:T(8,128)(2,1)} %all-gather.5.cloned.1.call-done) | copy-start | bytes 9437188
  348.6 5.5 copy-start
  550.0 1.4 copy-start.1
  550.0 1.9 copy-start.2
Sparse Core Ops, SparseCore 0:
  9.5 14.8 all-gather.4
  27.1 302.4 all-gather.6
  332.4 120.6 all-gather.8
  550.2 8.9 reduce-scatter.1
where the time goes:
time: 571 us; the launch traced here: 569 us
  waiting for transfers between devices  311 us (54%)
  matrix products  117 us (20%)
  local copies, waits for them, and re-layouts  73.2 us (13%)
  other arithmetic  41.3 us (7%)
  between operations  15.2 us (3%)
  loops' own time  9.17 us (2%)
    all_gather x1, waiting for transfers between devices, per_device(): lax.all_gather(qkv_weight, 'req', axis=1, tiled=True)  302 us
    dot_general x32, matrix products, score_block(): lax.dot_general(queries, key_rows, (((1,), (1,)), ((), ())), preferred_el...  57.1 us
    dynamic_slice x32, local copies, waits for them, and re-layouts, select(): return lax.dynamic_slice_in_dim(source, col_start, HD, 1)  40 us
    dot_general x16, matrix products, attend_whole(): jnp.dot(weights, value_rows, preferred_element_type=jnp.float32)  31.4 us
    dot_general x1, matrix products, add_rows(): jnp.einsum('td,jdc->jtc', source, piece, preferred_element_type=jnp.float32)  19 us
    reduce_sum x16, other arithmetic, attend_whole(): weights = (expo / jnp.sum(expo, axis=1, keepdims=True)).astype(jnp.bfloat16)  13.6 us
  transfers between devices with their start and end apart: 4, of which 3 were waited for; matrix products, arithmetic and copies ran while one was open for 38% of the time, Pallas kernels for 0%

commit v1 on v0

v1 whole, which is shorter than its diff:
```python
import functools
import math

import jax
import jax.numpy as jnp
from jax import lax
from jax.experimental import pallas as pl
from jax.experimental.pallas import tpu as pltpu
from jax.sharding import PartitionSpec as P

HD = 96
GROUP = 4 * HD

epsilon = 1e-05
masked_value = -1e30
theta_base = 10000.0


def rope_tables(positions):
    frequencies = jnp.power(theta_base, -jnp.arange(0, HD, 2, dtype=jnp.float32) / HD)
    angles = positions.astype(jnp.float32)[:, None] * jnp.tile(frequencies, 2)[None, :]
    sign = jnp.where(jnp.arange(HD) < HD // 2, -1.0, 1.0).astype(jnp.float32)
    return (
        jnp.tile(jnp.cos(angles), (1, GROUP // HD)),
        jnp.tile(jnp.sin(angles) * sign[None, :], (1, GROUP // HD)),
    )


def attend_kernel(span, cached, block, limits, proj, cos_ref, sin_ref, cache, att, entries, q_s):
    length = limits[0]
    valid = limits[1]
    cosine = cos_ref[...]
    sine = sin_ref[...]
    first = lax.broadcasted_iota(jnp.int32, (span, GROUP), 1) % HD < HD // 2

    def rotate(v):
        ahead = pltpu.roll(v, GROUP - HD // 2, 1)
        behind = pltpu.roll(v, HD // 2, 1)
        return v * cosine + jnp.where(first, ahead, behind) * sine

    q_s[0] = rotate(proj[0]).astype(jnp.bfloat16)
    q_s[1] = rotate(proj[1]).astype(jnp.bfloat16)
    q_s[2] = proj[2].astype(jnp.bfloat16)
    kept = lax.broadcasted_iota(jnp.int32, (span, GROUP), 0) < valid
    zeros = jnp.zeros((span, GROUP), jnp.float32)
    entries[0, 0] = jnp.where(kept, q_s[1].astype(jnp.float32), zeros).astype(jnp.bfloat16)
    entries[0, 1] = jnp.where(kept, q_s[2].astype(jnp.float32), zeros).astype(jnp.bfloat16)

    scale = math.log2(math.e) / math.sqrt(HD)
    cache_bias = jnp.where(
        lax.broadcasted_iota(jnp.int32, (1, cached), 1) < length, 0.0, masked_value
    )
    dims = (((1,), (1,)), ((), ()))
    for step in range(span // block):
        rows = slice(step * block, (step + 1) * block)
        seen = (step + 1) * block
        row_ids = lax.broadcasted_iota(jnp.int32, (block, seen), 0) + step * block
        col_ids = lax.broadcasted_iota(jnp.int32, (block, seen), 1)
        live = (col_ids <= row_ids) & (col_ids < valid)
        gathered = [None] * (GROUP // 128)
        for head in range(GROUP // HD):
            low = head * HD // 128 * 128
            high = -(-(head + 1) * HD // 128) * 128
            window = slice(low, high)
            lane = lax.broadcasted_iota(jnp.int32, (block, high - low), 1) + low
            mine = (lane >= head * HD) & (lane < (head + 1) * HD)
            query = jnp.where(mine, q_s[0, rows, window].astype(jnp.float32), 0.0).astype(
                jnp.bfloat16
            )
            old = (
                lax.dot_general(
                    query, cache[0, 0, :, window], dims, preferred_element_type=jnp.float32
                )
                * scale
                + cache_bias
            )
            new = (
                lax.dot_general(
                    query, q_s[1, :seen, window], dims, preferred_element_type=jnp.float32
                )
                * scale
            )
            new = jnp.where(live, new, masked_value)
            top = jnp.maximum(
                jnp.max(old, axis=1, keepdims=True), jnp.max(new, axis=1, keepdims=True)
            )
            old = jnp.exp2(old - top)
            new = jnp.exp2(new - top)
            total = jnp.sum(old, axis=1, keepdims=True) + jnp.sum(new, axis=1, keepdims=True)
            inverse = 1.0 / total
            result = jnp.dot(
                (old * inverse).astype(jnp.bfloat16),
                cache[0, 1, :, window],
                preferred_element_type=jnp.float32,
            ) + jnp.dot(
                (new * inverse).astype(jnp.bfloat16),
                q_s[2, :seen, window],
                preferred_element_type=jnp.float32,
            )
            result = jnp.where(mine, result, 0.0)
            for tile in range(low // 128, high // 128):
                piece = result[:, tile * 128 - low : (tile + 1) * 128 - low]
                gathered[tile] = piece if gathered[tile] is None else gathered[tile] + piece
        for tile, piece in enumerate(gathered):
            att[rows, tile * 128 : (tile + 1) * 128] = piece.astype(jnp.bfloat16)


def attend(limits, projected, cosine, sine, cache):
    _, span, cols = projected.shape
    cached = cache.shape[2]
    block = min(256, span)
    return pl.pallas_call(
        functools.partial(attend_kernel, span, cached, block),
        out_shape=(
            jax.ShapeDtypeStruct((span, cols), jnp.bfloat16),
            jax.ShapeDtypeStruct((1, 2, span, cols), jnp.bfloat16),
        ),
        grid_spec=pltpu.PrefetchScalarGridSpec(
            num_scalar_prefetch=1,
            grid=(cols // GROUP,),
            in_specs=[
                pl.BlockSpec((3, span, GROUP), lambda i, s: (0, 0, i)),
                pl.BlockSpec((span, GROUP), lambda i, s: (0, 0)),
                pl.BlockSpec((span, GROUP), lambda i, s: (0, 0)),
                pl.BlockSpec((1, 2, cached, GROUP), lambda i, s: (0, 0, 0, i)),
            ],
            out_specs=(
                pl.BlockSpec((span, GROUP), lambda i, s: (0, i)),
                pl.BlockSpec((1, 2, span, GROUP), lambda i, s: (0, 0, 0, i)),
            ),
            scratch_shapes=[pltpu.VMEM((3, span, GROUP), jnp.bfloat16)],
        ),
        compiler_params=pltpu.CompilerParams(vmem_limit_bytes=48 << 20),
        cost_estimate=pl.CostEstimate(
            flops=span * (cached + span) * cols * 8,
            bytes_accessed=cached * cols * 4 + span * cols * 20,
            transcendentals=span * (cached + span) * cols // HD,
        ),
        name="attend",
    )(limits, projected, cosine, sine, cache)


def gather_weights(mesh, qkv_weight):
    return lax.all_gather(qkv_weight, "req", axis=1, tiled=True)


def per_device(mesh, tokens, norm_gain, qkv_weight, out_weight, cache, cache_lens, valid_tokens):
    weights = gather_weights(mesh, qkv_weight)
    gathered, gain_all = (
        lax.all_gather(tokens, "tp", axis=1, tiled=True),
        lax.all_gather(norm_gain, "tp", axis=0, tiled=True),
    )
    inputs = gathered.astype(jnp.float32)
    spread = jnp.mean(inputs * inputs, axis=-1, keepdims=True)
    normed = (inputs * lax.rsqrt(spread + epsilon) * gain_all.astype(jnp.float32)).astype(
        jnp.bfloat16
    )
    token_ids = jnp.arange(normed.shape[0], dtype=jnp.int32)
    cosine, sine = rope_tables(cache_lens[0] + token_ids)
    projected = jnp.einsum("td,jdc->jtc", normed, weights, preferred_element_type=jnp.float32)
    turned, _ = lax.optimization_barrier((out_weight.T, weights[0, :8, :128]))
    out_all = lax.all_gather(turned, "req", axis=0, tiled=True)
    limits = jnp.concatenate([cache_lens, valid_tokens])
    attended, new_entries = attend(limits, projected, cosine, sine, cache)
    partial_value = lax.dot_general(
        attended, out_all, (((1,), (1,)), ((), ())), preferred_element_type=jnp.float32
    )
    summed = lax.psum_scatter(
        partial_value.astype(jnp.bfloat16), "tp", scatter_dimension=1, tiled=True
    ).astype(jnp.float32)
    kept = (token_ids < valid_tokens[0])[:, None]
    mixed_out = jnp.where(kept, summed, jnp.zeros_like(summed)).astype(jnp.bfloat16)
    return (mixed_out, new_entries)


def solution(mesh):
    placed = (
        P("req", "tp"),
        P("tp"),
        P(None, "req", "tp"),
        P("tp", "req"),
        P("req", None, None, "tp"),
        P("req"),
        P("req"),
    )
    return jax.shard_map(
        functools.partial(per_device, mesh),
        mesh=mesh,
        in_specs=placed,
        out_specs=(P("req", "tp"), P("req", None, None, "tp")),
        check_vma=False,
    )
```

time: 571 us -> 482 us (0.84)
  matrix products: 117 us -> 31.7 us
  local copies, waits for them, and re-layouts: 73.2 us -> 0.81 us
  waiting for transfers between devices: 311 us -> 382 us
  Pallas kernels: 0 us -> 43.6 us
  other arithmetic: 41.3 us -> 6.35 us
  loops' own time: 9.17 us -> 0 us
    dot_general x50 -> x2, matrix products: 117 us -> 31.7 us  [the longest x1 21.6 us: per_device(): jnp.einsum('td,jdc->jtc', normed, weights, preferred_element_type=jnp.flo...]
    all_gather x2, waiting for transfers between devices: 302 us -> 361 us  [the longest x1 303 us: gather_weights(): return lax.all_gather(qkv_weight, 'req', axis=1, tiled=True)]
    dynamic_slice x48 -> x0, local copies, waits for them, and re-layouts: 48.8 us -> none  [the longest x32 40 us: select(): return lax.dynamic_slice_in_dim(source, col_start, HD, 1)]
    pallas_call x0 -> x1, Pallas kernels: none -> 43.6 us  [attend(): pl.pallas_call(functools.partial(attend_kernel, span, cached, block), out...]
    reduce_sum x16 -> x0, other arithmetic: 13.6 us -> none  [attend_whole(): weights = (expo / jnp.sum(expo, axis=1, keepdims=True)).astype(jnp.bfloat16)]
    lt x17 -> x1, other arithmetic: 10.5 us -> 0.01 us  [per_device(): kept = (token_ids < valid_tokens[0])[:, None]]
    squeeze x1 -> x0, local copies, waits for them, and re-layouts: 10.4 us -> none  [per_device(): cache_values = cache[0, 1]]
    slice x3 -> x0, local copies, waits for them, and re-layouts: 9.36 us -> none  [the longest x2 6.98 us: per_device(): projected[1]]
  transfers between devices with their start and end apart: 4 -> 4, of which waited for: 3 -> 4; matrix products, arithmetic and copies ran while one was open for 38% -> 5% of each run, Pallas kernels for 0% -> 9%
where the time goes in v1:
time: 482 us
  waiting for transfers between devices  382 us (79%)
  Pallas kernels  43.6 us (9%)
  matrix products  31.7 us (7%)
  between operations  15.1 us (3%)
  other arithmetic  6.35 us (1%)
    all_gather x1, waiting for transfers between devices, gather_weights(): return lax.all_gather(qkv_weight, 'req', axis=1, tiled=True)  303 us
    all_gather x1, waiting for transfers between devices, per_device(): out_all = lax.all_gather(turned, 'req', axis=0, tiled=True)  58.3 us
    pallas_call x1, Pallas kernels, attend(): pl.pallas_call(functools.partial(attend_kernel, span, cached, block), out...  43.6 us
    dot_general x1, matrix products, per_device(): jnp.einsum('td,jdc->jtc', normed, weights, preferred_element_type=jnp.flo...  21.6 us
    dot_general x1, matrix products, per_device(): lax.dot_general(attended, out_all, (((1,), (1,)), ((), ())), preferred_el...  10.1 us
    all_gather x1, waiting for transfers between devices, per_device(): lax.all_gather(tokens, 'tp', axis=1, tiled=True)  9.98 us
  transfers between devices with their start and end apart: 4, of which 4 were waited for; matrix products, arithmetic and copies ran while one was open for 5% of the time, Pallas kernels for 9%

profile of v1, /device:TPU:0, one launch (start us, length us, event | category | flops | bytes accessed | tf_op | source)
XLA Modules:
  0.0 481.9 jit_solution(8296177296244336988)
XLA Ops:
  7.2 0.0 copy-start
  7.2 0.0 all-gather.5.cloned.1.call-start
  7.2 0.7 all-gather.5.cloned.1.call-update
  7.9 0.0 all-gather.7.cloned.1.call-start
  8.0 0.7 all-gather.7.cloned.1.call-update
  8.7 0.0 all-gather.9.cloned.1.call-start
  8.7 0.7 all-gather.9.cloned.1.call-update
  9.4 0.0 reduce-scatter.2.cloned.1.call-start
  9.4 0.0 copy-done
  9.5 1.9 all-gather
  12.1 0.1 mul.71
  12.2 0.8 fusion.7
  13.0 0.1 tile.11
  13.1 0.3 copy.11.cos_ref
  13.3 0.1 tile.13
  13.4 0.3 copy.12.sin_ref
  14.3 0.1 pad_add_fusion.limits
  14.4 10.0 %all-gather.5.cloned.1.call-done = bf16[512,3072]{1,0:T(8,128)(2,1)} async-done(((bf16[512,1536]{1,0:T(8,128)(2,1)}), bf16[512,3072]{1,0:T(8,128)(2,1)}) %all-gather.5.cloned.1.call-update) | async-done | bytes 3145744 | tf_op jit(solution)/shard_map/all_gather | solution.py:150
  24.4 2.6 fusion
  27.0 302.6 %all-gather.7.cloned.1.call-done = bf16[3,3072,1536]{2,1,0:T(8,128)(2,1)} async-done(((bf16[3,192,1536]{2,1,0:T(8,128)(2,1)}), bf16[3,3072,1536]{2,1,0:T(8,128)(2,1)}) %all-gather.7.cloned.1.call-update) | async-done | bytes 28311568 | tf_op jit(solution)/shard_map/all_gather | solution.py:144
  329.6 21.6 %convolution_bitcast_fusion.proj = f32[3,512,1536]{2,1,0:T(8,128)} fusion(bf16[3,3072,1536]{2,1,0:T(8,128)(2,1)} %all-gather.7.cloned.1.call-done, bf16[512,3072]{1,0:T(8,128)(2,1)} %all-gather.5.cloned.1.call-done, f32[3072]{0:T(1024)S(1)} %bitcast.19, f32[512]{0:T(512)S(1)} %add_rsqrt_fusion), kind=kOutput, calls=%fused_computation.5 | convolution fusion | flops 14501806080 | bytes 40908800 | tf_op jit(solution)/shard_map/td,jdc->jtc/dot_general | solution.py:160
  351.2 43.6 %attend.1 = (bf16[512,1536]{1,0:T(8,128)(2,1)S(1)}, bf16[1,2,512,1536]{3,2,1,0:T(8,128)(2,1)}) custom-call(s32[2]{0:T(128)S(1)} %pad_add_fusion.limits, f32[3,512,1536]{2,1,0:T(8,128)} %convolution_bitcast_fusion.proj, f32[512,384]{1,0:T(8,128)S(1)} %copy.11.cos_ref, f32[512,384]{1,0:T(8,128)S(1)} %copy.12.sin_ref, bf16[1,2,2048,1536]{3,2,1,0:T(8,128)(2,1)} %cache.1), custom_call_target="tpu_custom_call" | custom-call | flops 16106127360 | bytes 28311552 | tf_op jit(solution)/shard_map/attend/pallas_call | solution.py:112
  394.8 58.3 %all-gather.9.cloned.1.call-done = bf16[3072,1536]{1,0:T(8,128)(2,1)} async-done(((bf16[192,1536]{1,0:T(8,128)(2,1)}), bf16[3072,1536]{1,0:T(8,128)(2,1)}) %all-gather.9.cloned.1.call-update) | async-done | bytes 9437200 | tf_op jit(solution)/shard_map/all_gather | solution.py:162
  453.1 10.1 %convolution_convert_fusion = bf16[512,3072]{1,0:T(8,128)(2,1)} fusion(bf16[512,1536]{1,0:T(8,128)(2,1)S(1)} %get-tuple-element.4, bf16[3072,1536]{1,0:T(8,128)(2,1)} %all-gather.9.cloned.1.call-done), kind=kOutput, calls=%fused_computation.6 | convolution fusion | flops 4833411072 | bytes 14155776 | tf_op jit(solution)/shard_map/dot_general | solution.py:165
  463.2 0.0 reduce-scatter.2.cloned.1.call-update
  463.2 9.2 %reduce-scatter.2.cloned.1.call-done = bf16[512,1536]{1,0:T(8,128)(2,1)} async-done(((bf16[512,3072]{1,0:T(8,128)(2,1)}), bf16[512,1536]{1,0:T(8,128)(2,1)}) %reduce-scatter.2.cloned.1.call-update) | async-done | bytes 1572880 | tf_op jit(solution)/shard_map/reduce_scatter | solution.py:168
  472.5 2.9 select_convert_fusion
  (8 shorter events, 0.1 us)
Async XLA Ops:
  7.2 2.3 copy-start
  7.2 17.2 %all-gather.5.cloned.1.call-start = ((), (), s32[]{:S(2)}) async-start(), calls=%async_computation.1 | async-start | bytes 4718592 | tf_op jit(solution)/shard_map/all_gather | solution.py:150
  7.9 321.7 %all-gather.7.cloned.1.call-start = ((), (), s32[]{:S(2)}) async-start(), calls=%async_computation.2 | async-start | bytes 30081024 | tf_op jit(solution)/shard_map/all_gather | solution.py:144
  8.7 444.5 %all-gather.9.cloned.1.call-start = ((), (), s32[]{:S(2)}) async-start(), calls=%async_computation.3 | async-start | bytes 10027008 | tf_op jit(solution)/shard_map/all_gather | solution.py:162
  9.4 463.1 %reduce-scatter.2.cloned.1.call-start = ((), (), s32[]{:S(2)}) async-start(), calls=%async_computation.4 | async-start | bytes 4718592 | tf_op jit(solution)/shard_map/reduce_scatter | solution.py:168
Sparse Core Ops, SparseCore 0:
  9.5 14.8 all-gather.4
  27.1 302.4 all-gather.6
  332.4 120.6 all-gather.8
  463.4 9.0 reduce-scatter.1

commit v2 on v1

--- a/solution.py
+++ b/solution.py
@@ -140,8 +140,135 @@
     )(limits, projected, cosine, sine, cache)
 
 
-def gather_weights(mesh, qkv_weight):
-    return lax.all_gather(qkv_weight, "req", axis=1, tiled=True)
+def gather_events():
+    events = []
+    for stream, order in enumerate(("xyz", "zyx", "zxy")):
+        for dz in range(-3, 4):
+            for dy in range(2):
+                for dx in range(2):
+                    offset = {"z": dz, "y": dy, "x": dx}
+                    moved = [axis for axis in order if offset[axis]]
+                    if moved:
+                        hops = abs(dz) + dy + dx
+                        events.append((hops, order.index(moved[-1]), stream, moved[-1], dz, dy, dx))
+    events.sort()
+    return [(stream, via, dz, dy, dx) for _, _, stream, via, dz, dy, dx in events]
+
+
+def gather_kernel(cuts, shard, full, send_sem, recv_sem, own_sem):
+    me = lax.axis_index("req")
+    core = lax.axis_index("tp")
+    z, y, x = lax.div(me, 4), lax.rem(lax.div(me, 2), 2), lax.rem(me, 2)
+    beside = {"x": me + 1 - 2 * x, "y": me + 2 - 4 * y}
+    orders = ("xyz", "zyx", "zxy")
+
+    barrier = pltpu.get_barrier_semaphore()
+
+    def greet(target):
+        pl.semaphore_signal(
+            barrier, inc=1, device_id=(target, core), device_id_type=pl.DeviceIdType.MESH
+        )
+
+    greet(beside["x"])
+    greet(beside["y"])
+
+    @pl.when(z < 3)
+    def _():
+        greet(me + 4)
+
+    @pl.when(z > 0)
+    def _():
+        greet(me - 4)
+
+    inner = jnp.where(z > 0, 1, 0) + jnp.where(z < 3, 1, 0)
+    pl.semaphore_wait(barrier, 2 + inner)
+
+    def block(ref, stream, source):
+        return ref.at[:, source, cuts[stream] : cuts[stream + 1], :]
+
+    def copy(stream, source, lane, target, own):
+        there = block(full, stream, source)
+        here = shard.at[:, cuts[stream] : cuts[stream + 1], :] if own else there
+        return pltpu.make_async_remote_copy(
+            src_ref=here,
+            dst_ref=there,
+            send_sem=send_sem.at[stream, source, lane],
+            recv_sem=recv_sem.at[stream, source],
+            device_id=(target, core),
+            device_id_type=pl.DeviceIdType.MESH,
+        )
+
+    def forward(stream, source, via, dz, own, act):
+        order = orders[stream]
+        for axis in order[order.index(via) if via else 0 :]:
+            if axis == "z":
+                if not via or dz < 0 or via != "z":
+
+                    @pl.when(z < 3)
+                    def _():
+                        act(copy(stream, source, 0, me + 4, own))
+
+                if not via or dz > 0 or via != "z":
+
+                    @pl.when(z > 0)
+                    def _():
+                        act(copy(stream, source, 1, me - 4, own))
+
+            elif axis != via:
+                lane = 2 if axis == "y" else 3
+                act(copy(stream, source, lane, beside[axis], own))
+
+    for stream in (1, 2, 0):
+        forward(stream, me, None, 0, True, lambda c: c.start())
+    kept = pltpu.make_async_copy(shard, full.at[:, me], own_sem)
+    kept.start()
+
+    def visit(event, act, arrived):
+        stream, via, dz, dy, dx = event
+        source = me + 4 * dz + dy * (2 - 4 * y) + dx * (1 - 2 * x)
+
+        def body():
+            if arrived:
+                copy(stream, source, 0, beside["x"], False).wait_recv()
+            forward(stream, source, via, dz, False, act)
+
+        if dz > 0:
+            pl.when(z + dz <= 3)(body)
+        elif dz < 0:
+            pl.when(z + dz >= 0)(body)
+        else:
+            body()
+
+    for event in gather_events():
+        visit(event, lambda c: c.start(), True)
+    for stream in (1, 2, 0):
+        forward(stream, me, None, 0, True, lambda c: c.wait_send())
+    for event in gather_events():
+        visit(event, lambda c: c.wait_send(), False)
+    kept.wait()
+
+
+def gather_weights(mesh, shard):
+    peers = mesh.shape["req"]
+    count, rows, cols = shard.shape
+    if peers != 16 or rows % 192:
+        return lax.all_gather(shard, "req", axis=1, tiled=True)
+    unit = rows // 12
+    cuts = (0, 2 * unit, 7 * unit, rows)
+    full = pl.pallas_call(
+        functools.partial(gather_kernel, cuts),
+        out_shape=jax.ShapeDtypeStruct((count, peers, rows, cols), shard.dtype),
+        in_specs=[pl.BlockSpec(memory_space=pl.ANY)],
+        out_specs=pl.BlockSpec(memory_space=pl.ANY),
+        scratch_shapes=[
+            pltpu.SemaphoreType.DMA((3, peers, 4)),
+            pltpu.SemaphoreType.DMA((3, peers)),
+            pltpu.SemaphoreType.DMA,
+        ],
+        compiler_params=pltpu.CompilerParams(collective_id=0, has_side_effects=True),
+        name="gather_weights",
+    )(shard)
+    return full.reshape(count, peers * rows, cols)
 
 
 def per_device(mesh, tokens, norm_gain, qkv_weight, out_weight, cache, cache_lens, valid_tokens):

time: 482 us -> 378 us (0.78)
  waiting for transfers between devices: 382 us -> 12.5 us
  Pallas kernels: 43.6 us -> 310 us
    all_gather x1 -> x0, waiting for transfers between devices: 303 us -> none  [gather_weights(): return lax.all_gather(qkv_weight, 'req', axis=1, tiled=True)]
    pallas_call x0 -> x1, Pallas kernels: none -> 267 us  [gather_weights(): pl.pallas_call(functools.partial(gather_kernel, cuts), out_shape=jax.Shap...]
    all_gather x1, waiting for transfers between devices: 58.3 us -> 0.01 us  [per_device(): out_all = lax.all_gather(turned, 'req', axis=0, tiled=True)]
    all_gather x1, waiting for transfers between devices: 9.98 us -> 0.01 us  [per_device(): lax.all_gather(tokens, 'tp', axis=1, tiled=True)]
  transfers between devices with their start and end apart: 4 -> 3, of which waited for: 4 -> 1; matrix products, arithmetic and copies ran while one was open for 5% -> 7% of each run, Pallas kernels for 9% -> 82%
where the time goes in v2:
time: 378 us
  Pallas kernels  310 us (82%)
  matrix products  30.9 us (8%)
  between operations  15.1 us (4%)
  waiting for transfers between devices  12.5 us (3%)
  other arithmetic  6.49 us (2%)
    pallas_call x1, Pallas kernels, gather_weights(): pl.pallas_call(functools.partial(gather_kernel, cuts), out_shape=jax.Shap...  267 us
    pallas_call x1, Pallas kernels, attend(): pl.pallas_call(functools.partial(attend_kernel, span, cached, block), out...  43.6 us
    dot_general x1, matrix products, per_device(): jnp.einsum('td,jdc->jtc', normed, weights, preferred_element_type=jnp.flo...  20.8 us
    reduce_scatter x1, waiting for transfers between devices, per_device(): lax.psum_scatter(partial_value.astype(jnp.bfloat16), 'tp', scatter_dimens...  11.2 us
    dot_general x1, matrix products, per_device(): lax.dot_general(attended, out_all, (((1,), (1,)), ((), ())), preferred_el...  10.1 us
  transfers between devices with their start and end apart: 3, of which 1 were waited for; matrix products, arithmetic and copies ran while one was open for 7% of the time, Pallas kernels for 82%

profile of v2, /device:TPU:0, one launch (start us, length us, event | category | flops | bytes accessed | tf_op | source)
XLA Modules:
  0.0 378.2 jit_solution(10333519858427519868)
XLA Ops:
  7.2 0.0 all-gather.4.cloned.1.call-start
  7.2 0.7 all-gather.4.cloned.1.call-update
  7.9 0.0 all-gather.6.cloned.1.call-start
  7.9 0.7 all-gather.6.cloned.1.call-update
  8.6 0.0 copy-start.1
  8.7 0.0 reduce-scatter.2.cloned.1.call-start
  8.7 266.8 %gather_weights.1 = bf16[3,16,192,1536]{3,2,1,0:T(8,128)(2,1)} custom-call(bf16[3,192,1536]{2,1,0:T(8,128)(2,1)} %shard.1), custom_call_target="tpu_custom_call" | custom-call | tf_op jit(solution)/shard_map/gather_weights/pallas_call | solution.py:258
  275.5 0.0 copy-done.1
  275.5 1.8 all-gather
  278.0 0.1 mul.71
  278.1 0.8 fusion.7
  278.9 0.1 tile.11
  279.0 0.3 copy.11.cos_ref
  279.2 0.1 tile.13
  279.3 0.3 copy.12.sin_ref
  280.2 0.1 pad_add_fusion.limits
  280.3 0.0 all-gather.4.cloned.1.call-done
  280.3 0.0 copy-start
  280.3 2.7 fusion
  283.1 0.1 copy-done
  283.2 20.8 %convolution_bitcast_fusion.proj = f32[3,512,1536]{2,1,0:T(8,128)} fusion(bf16[3,3072,1536]{2,1,0:T(8,128)(2,1)} %bitcast.17, bf16[512,3072]{1,0:T(8,128)(2,1)S(1)} %copy-done, f32[3072]{0:T(1024)S(1)} %bitcast.21, f32[512]{0:T(512)S(1)} %add_rsqrt_fusion), kind=kOutput, calls=%fused_computation.5 | convolution fusion | flops 14501806080 | bytes 40908800 | tf_op jit(solution)/shard_map/td,jdc->jtc/dot_general | solution.py:287
  303.9 43.6 %attend.1 = (bf16[512,1536]{1,0:T(8,128)(2,1)S(1)}, bf16[1,2,512,1536]{3,2,1,0:T(8,128)(2,1)}) custom-call(s32[2]{0:T(128)S(1)} %pad_add_fusion.limits, f32[3,512,1536]{2,1,0:T(8,128)} %convolution_bitcast_fusion.proj, f32[512,384]{1,0:T(8,128)S(1)} %copy.11.cos_ref, f32[512,384]{1,0:T(8,128)S(1)} %copy.12.sin_ref, bf16[1,2,2048,1536]{3,2,1,0:T(8,128)(2,1)} %cache.1), custom_call_target="tpu_custom_call" | custom-call | flops 16106127360 | bytes 28311552 | tf_op jit(solution)/shard_map/attend/pallas_call | solution.py:112
  347.5 0.0 all-gather.6.cloned.1.call-done
  347.5 10.1 %convolution_convert_fusion = bf16[512,3072]{1,0:T(8,128)(2,1)} fusion(bf16[512,1536]{1,0:T(8,128)(2,1)S(1)} %get-tuple-element.4, bf16[3072,1536]{1,0:T(8,128)(2,1)} %all-gather.6.cloned.1.call-done), kind=kOutput, calls=%fused_computation.6 | convolution fusion | flops 4833411072 | bytes 14155776 | tf_op jit(solution)/shard_map/dot_general | solution.py:292
  357.6 0.0 reduce-scatter.2.cloned.1.call-update
  357.7 11.2 %reduce-scatter.2.cloned.1.call-done = bf16[512,1536]{1,0:T(8,128)(2,1)} async-done(((bf16[512,3072]{1,0:T(8,128)(2,1)}), bf16[512,1536]{1,0:T(8,128)(2,1)}) %reduce-scatter.2.cloned.1.call-update) | async-done | bytes 1572880 | tf_op jit(solution)/shard_map/reduce_scatter | solution.py:295
  368.8 2.9 select_convert_fusion
  (8 shorter events, 0.1 us)
Async XLA Ops:
  7.2 273.2 %all-gather.4.cloned.1.call-start = ((), (), s32[]{:S(2)}) async-start(), calls=%async_computation.1 | async-start | bytes 4718592 | tf_op jit(solution)/shard_map/all_gather | solution.py:277
  7.9 339.6 %all-gather.6.cloned.1.call-start = ((), (), s32[]{:S(2)}) async-start(), calls=%async_computation.2 | async-start | bytes 10027008 | tf_op jit(solution)/shard_map/all_gather | solution.py:289
  8.6 266.8 %copy-start.1 = (bf16[1536]{0:T(1024)(128)(2,1)S(1)}, bf16[1536]{0:T(1024)(128)(2,1)}, u32[]{:S(2)}) copy-start(bf16[1536]{0:T(1024)(128)(2,1)} %param.8) | copy-start | bytes 9220
  8.7 360.2 %reduce-scatter.2.cloned.1.call-start = ((), (), s32[]{:S(2)}) async-start(), calls=%async_computation.3 | async-start | bytes 4718592 | tf_op jit(solution)/shard_map/reduce_scatter | solution.py:295
  280.3 2.8 copy-start
Sparse Core Ops, SparseCore 0:
  9.5 14.8 all-gather.3
  27.2 199.3 all-gather.5
  357.8 10.9 reduce-scatter.1

commit v3 on v2

--- a/solution.py
+++ b/solution.py
@@ -155,7 +155,7 @@
     return [(stream, via, dz, dy, dx) for _, _, stream, via, dz, dy, dx in events]
 
 
-def gather_kernel(cuts, shard, full, send_sem, recv_sem, own_sem):
+def gather_kernel(cuts, shard, later, full, released, send_sem, recv_sem, own_sem, later_sem):
     me = lax.axis_index("req")
     core = lax.axis_index("tp")
     z, y, x = lax.div(me, 4), lax.rem(lax.div(me, 2), 2), lax.rem(me, 2)
@@ -222,6 +222,8 @@
         forward(stream, me, None, 0, True, lambda c: c.start())
     kept = pltpu.make_async_copy(shard, full.at[:, me], own_sem)
     kept.start()
+    held = pltpu.make_async_copy(later, released, later_sem)
+    held.start()
 
     def visit(event, act, arrived):
         stream, via, dz, dy, dx = event
@@ -246,33 +248,42 @@
     for event in gather_events():
         visit(event, lambda c: c.wait_send(), False)
     kept.wait()
-
-
-def gather_weights(mesh, shard):
+    held.wait()
+
+
+def gather_weights(mesh, shard, later):
     peers = mesh.shape["req"]
     count, rows, cols = shard.shape
     if peers != 16 or rows % 192:
-        return lax.all_gather(shard, "req", axis=1, tiled=True)
+        return lax.all_gather(shard, "req", axis=1, tiled=True), later
     unit = rows // 12
     cuts = (0, 2 * unit, 7 * unit, rows)
-    full = pl.pallas_call(
+    full, released = pl.pallas_call(
         functools.partial(gather_kernel, cuts),
-        out_shape=jax.ShapeDtypeStruct((count, peers, rows, cols), shard.dtype),
-        in_specs=[pl.BlockSpec(memory_space=pl.ANY)],
-        out_specs=pl.BlockSpec(memory_space=pl.ANY),
+        out_shape=(
+            jax.ShapeDtypeStruct((count, peers, rows, cols), shard.dtype),
+            jax.ShapeDtypeStruct(later.shape, later.dtype),
+        ),
+        in_specs=[pl.BlockSpec(memory_space=pl.ANY)] * 2,
+        out_specs=(pl.BlockSpec(memory_space=pl.ANY),) * 2,
         scratch_shapes=[
             pltpu.SemaphoreType.DMA((3, peers, 4)),
             pltpu.SemaphoreType.DMA((3, peers)),
             pltpu.SemaphoreType.DMA,
+            pltpu.SemaphoreType.DMA,
         ],
         compiler_params=pltpu.CompilerParams(collective_id=0, has_side_effects=True),
         name="gather_weights",
-    )(shard)
-    return full.reshape(count, peers * rows, cols)
+    )(shard, later)
+    return full.reshape(count, peers * rows, cols), released
 
 
 def per_device(mesh, tokens, norm_gain, qkv_weight, out_weight, cache, cache_lens, valid_tokens):
-    weights = gather_weights(mesh, qkv_weight)
+    turned = out_weight.T
+    cut = turned.shape[1] * 5 // 12 // 128 * 128
+    out_early = lax.all_gather(turned[:, :cut], "req", axis=0, tiled=True)
+    weights, released = gather_weights(mesh, qkv_weight, turned[:, cut:])
+    out_late = lax.all_gather(released, "req", axis=0, tiled=True)
     gathered, gain_all = (
         lax.all_gather(tokens, "tp", axis=1, tiled=True),
         lax.all_gather(norm_gain, "tp", axis=0, tiled=True),
@@ -285,12 +296,13 @@
     token_ids = jnp.arange(normed.shape[0], dtype=jnp.int32)
     cosine, sine = rope_tables(cache_lens[0] + token_ids)
     projected = jnp.einsum("td,jdc->jtc", normed, weights, preferred_element_type=jnp.float32)
-    turned, _ = lax.optimization_barrier((out_weight.T, weights[0, :8, :128]))
-    out_all = lax.all_gather(turned, "req", axis=0, tiled=True)
     limits = jnp.concatenate([cache_lens, valid_tokens])
     attended, new_entries = attend(limits, projected, cosine, sine, cache)
+    rows_dims = (((1,), (1,)), ((), ()))
     partial_value = lax.dot_general(
-        attended, out_all, (((1,), (1,)), ((), ())), preferred_element_type=jnp.float32
+        attended[:, :cut], out_early, rows_dims, preferred_element_type=jnp.float32
+    ) + lax.dot_general(
+        attended[:, cut:], out_late, rows_dims, preferred_element_type=jnp.float32
     )
     summed = lax.psum_scatter(
         partial_value.astype(jnp.bfloat16), "tp", scatter_dimension=1, tiled=True

time: 378 us -> 357 us (0.944)
  Pallas kernels: 310 us -> 274 us
  matrix products: 30.9 us -> 37.1 us
  waiting for transfers between devices: 12.5 us -> 17.2 us
    pallas_call x1, Pallas kernels: 267 us -> 231 us  [gather_weights(): pl.pallas_call(functools.partial(gather_kernel, cuts), out_shape=(jax.Sha...]
    all_gather x1 -> x2, waiting for transfers between devices: 0.01 us -> 6.97 us  [the longest x1 6.97 us: per_device(): out_late = lax.all_gather(released, 'req', axis=0, tiled=True)]
    dot_general x1 -> x2, matrix products: 10.1 us -> 15.3 us  [the longest x1 8.54 us: per_device(): lax.dot_general(attended[:, cut:], out_late, rows_dims, preferred_element...]
  transfers between devices with their start and end apart: 3 -> 4, of which waited for: 1 -> 2; matrix products, arithmetic and copies ran while one was open for 7% -> 10% of each run, Pallas kernels for 82% -> 77%
where the time goes in v3:
time: 357 us; the launch traced here: 356 us
  Pallas kernels  274 us (77%)
  matrix products  37.1 us (10%)
  waiting for transfers between devices  17.2 us (5%)
  between operations  15.1 us (4%)
  other arithmetic  6.35 us (2%)
  local copies, waits for them, and re-layouts  4.21 us (1%)
    pallas_call x1, Pallas kernels, gather_weights(): pl.pallas_call(functools.partial(gather_kernel, cuts), out_shape=(jax.Sha...  231 us
    pallas_call x1, Pallas kernels, attend(): pl.pallas_call(functools.partial(attend_kernel, span, cached, block), out...  43.6 us
    dot_general x1, matrix products, per_device(): jnp.einsum('td,jdc->jtc', normed, weights, preferred_element_type=jnp.flo...  21.8 us
    reduce_scatter x1, waiting for transfers between devices, per_device(): lax.psum_scatter(partial_value.astype(jnp.bfloat16), 'tp', scatter_dimens...  9.5 us
    dot_general x1, matrix products, per_device(): lax.dot_general(attended[:, cut:], out_late, rows_dims, preferred_element...  8.54 us
  transfers between devices with their start and end apart: 4, of which 2 were waited for; matrix products, arithmetic and copies ran while one was open for 10% of the time, Pallas kernels for 77%

profile of v3, /device:TPU:0, one launch (start us, length us, event | category | flops | bytes accessed | tf_op | source)
XLA Modules:
  0.0 356.3 jit_solution(9910720964276905565)
XLA Ops:
  7.2 0.0 copy-start
  7.2 0.0 all-gather.5.cloned.1.call-start
  7.2 0.7 all-gather.5.cloned.1.call-update
  7.9 0.0 all-gather.7.cloned.1.call-start
  8.0 1.7 slice.17
  9.6 0.0 all-gather.7.cloned.1.call-update
  9.6 0.0 all-gather.9.cloned.1.call-start
  9.7 1.7 slice.16.later
  11.4 230.8 %gather_weights.1 = (bf16[3,16,192,1536]{3,2,1,0:T(8,128)(2,1)}, bf16[192,896]{1,0:T(8,128)(2,1)}) custom-call(bf16[3,192,1536]{2,1,0:T(8,128)(2,1)} %shard.1, bf16[192,896]{1,0:T(8,128)(2,1)} %slice.16.later), custom_call_target="tpu_custom_call" | custom-call | tf_op jit(solution)/shard_map/gather_weights/pallas_call | solution.py:261
  242.2 0.0 all-gather.9.cloned.1.call-update
  242.2 0.0 reduce-scatter.2.cloned.1.call-start
  242.3 0.0 copy-done
  242.3 1.8 all-gather
  244.8 0.1 mul.71
  244.9 0.8 fusion.10
  245.7 0.1 tile.11
  245.7 0.3 copy.17.cos_ref
  246.0 0.1 tile.13
  246.1 0.3 copy.18.sin_ref
  247.0 0.1 pad_add_fusion.limits
  247.1 0.0 all-gather.5.cloned.1.call-done
  247.1 2.6 fusion
  249.7 21.8 %convolution_bitcast_fusion.proj = f32[3,512,1536]{2,1,0:T(8,128)} fusion(bf16[3,3072,1536]{2,1,0:T(8,128)(2,1)} %bitcast.22, bf16[512,3072]{1,0:T(8,128)(2,1)} %all-gather.5.cloned.1.call-done, f32[3072]{0:T(1024)S(1)} %bitcast.21, f32[512]{0:T(512)S(1)} %add_rsqrt_fusion), kind=kOutput, calls=%fused_computation.6 | convolution fusion | flops 14501806080 | bytes 40908800 | tf_op jit(solution)/shard_map/td,jdc->jtc/dot_general | solution.py:298
  271.5 43.6 %attend.1 = (bf16[512,1536]{1,0:T(8,128)(2,1)S(1)}, bf16[1,2,512,1536]{3,2,1,0:T(8,128)(2,1)}) custom-call(s32[2]{0:T(128)S(1)} %pad_add_fusion.limits, f32[3,512,1536]{2,1,0:T(8,128)} %convolution_bitcast_fusion.proj, f32[512,384]{1,0:T(8,128)S(1)} %copy.17.cos_ref, f32[512,384]{1,0:T(8,128)S(1)} %copy.18.sin_ref, bf16[1,2,2048,1536]{3,2,1,0:T(8,128)(2,1)} %cache.1), custom_call_target="tpu_custom_call" | custom-call | flops 16106127360 | bytes 28311552 | tf_op jit(solution)/shard_map/attend/pallas_call | solution.py:112
  315.1 0.0 all-gather.7.cloned.1.call-done
  315.1 6.8 %fusion.8 = f32[512,3072]{1,0:T(8,128)} fusion(bf16[3072,640]{1,0:T(8,128)(2,1)} %all-gather.7.cloned.1.call-done, bf16[512,1536]{1,0:T(8,128)(2,1)S(1)} %get-tuple-element.7), kind=kOutput, calls=%fused_computation.12 | convolution fusion | flops 2013265920 | bytes 10878976 | tf_op jit(solution)/shard_map/dot_general | solution.py:302
  321.9 7.0 %all-gather.9.cloned.1.call-done = bf16[3072,896]{1,0:T(8,128)(2,1)} async-done(((bf16[192,896]{1,0:T(8,128)(2,1)}), bf16[3072,896]{1,0:T(8,128)(2,1)}) %all-gather.9.cloned.1.call-update) | async-done | bytes 5505040 | tf_op jit(solution)/shard_map/all_gather | solution.py:286
  328.9 8.5 %add_convert_fusion = bf16[512,3072]{1,0:T(8,128)(2,1)} fusion(f32[512,3072]{1,0:T(8,128)} %fusion.8, bf16[3072,896]{1,0:T(8,128)(2,1)} %all-gather.9.cloned.1.call-done, bf16[512,1536]{1,0:T(8,128)(2,1)S(1)} %get-tuple-element.7), kind=kOutput, calls=%fused_computation.5 | convolution fusion | flops 2821718016 | bytes 15859712 | tf_op jit(solution)/shard_map/dot_general | solution.py:304
  337.4 0.0 reduce-scatter.2.cloned.1.call-update
  337.4 9.5 %reduce-scatter.2.cloned.1.call-done = bf16[512,1536]{1,0:T(8,128)(2,1)} async-done(((bf16[512,3072]{1,0:T(8,128)(2,1)}), bf16[512,1536]{1,0:T(8,128)(2,1)}) %reduce-scatter.2.cloned.1.call-update) | async-done | bytes 1572880 | tf_op jit(solution)/shard_map/reduce_scatter | solution.py:307
  346.9 2.9 select_convert_fusion
  (8 shorter events, 0.1 us)
Async XLA Ops:
  7.2 235.1 %copy-start = (bf16[1536]{0:T(1024)(128)(2,1)S(1)}, bf16[1536]{0:T(1024)(128)(2,1)}, u32[]{:S(2)}) copy-start(bf16[1536]{0:T(1024)(128)(2,1)} %param.8) | copy-start | bytes 9220
  7.2 239.9 %all-gather.5.cloned.1.call-start = ((), (), s32[]{:S(2)}) async-start(), calls=%async_computation.1 | async-start | bytes 4718592 | tf_op jit(solution)/shard_map/all_gather | solution.py:288
  7.9 307.2 %all-gather.7.cloned.1.call-start = ((), (), s32[]{:S(2)}) async-start(), calls=%async_computation.2 | async-start | bytes 4177920 | tf_op jit(solution)/shard_map/all_gather | solution.py:284
  9.6 319.2 %all-gather.9.cloned.1.call-start = ((), (), s32[]{:S(2)}) async-start(), calls=%async_computation.3 | async-start | bytes 5849088 | tf_op jit(solution)/shard_map/all_gather | solution.py:286
  242.2 104.7 %reduce-scatter.2.cloned.1.call-start = ((), (), s32[]{:S(2)}) async-start(), calls=%async_computation.4 | async-start | bytes 4718592 | tf_op jit(solution)/shard_map/reduce_scatter | solution.py:307
Sparse Core Ops, SparseCore 0:
  9.5 14.8 all-gather.4
  27.2 105.8 all-gather.6
  242.3 86.4 all-gather.8
  337.5 9.3 reduce-scatter.1
